TPU v7x, 32 devices: a whole 2x2x4 slice. The times are simulated.
32 devices in a mesh: layer: 4 (over z), row: 2 (over x), col: 4 (over y, core).
Axes of the slice: x: 2, y: 2, z: 4, core: 2. Of those that a mesh axis runs over, the one named last changes fastest.
Arguments:
- cost_vector: float32 [8, 1024, 512], P('layer', 'row', 'col'), may hold values from -12 to 12
- metal_density: float32 [8, 1024, 512], P('layer', 'row', 'col'), may hold values from 0 to 0.5
- cap_class: int32 [8, 1024, 512], P('layer', 'row', 'col'), may hold values from 0 to 7
- blocked_mask: int32 [8, 1024, 512], P('layer', 'row', 'col'), may hold values 0 or 1
- fill_start: float32 [8, 1024, 512], P('layer', 'row', 'col'), may hold values from 0 to 1
- window_dual: float32 [8, 1024, 512], P('layer', 'row', 'col'), may hold values from -4 to 4
- layer_dual: float32 [8, 1024, 512], P('layer', 'row', 'col'), may hold values from -4 to 4
Outputs:
- fill_level: float32 [8, 1024, 512], P('layer', 'row', 'col')
- window_price: float32 [8, 1024, 512], P('layer', 'row', 'col')
- layer_price: float32 [8, 1024, 512], P('layer', 'row', 'col')
- primal_weight: float32 [], replicated
All inputs are finite; a program needn't handle non-finite values. No bound on the sum of `blocked_mask` on one device may be relied on, other than what follows from the above.
Results may differ from a plain program's by a relative error of at most 0.00011.
Values sent between devices are 32-bit elements; how exact they have to be, the bound alone decides.
A program may use at most 64 MiB of HBM per device.

v0:
```python
import jax
import jax.numpy as jnp
from jax import lax
from jax.sharding import PartitionSpec as P

WIN = 50
CAP_LEVELS = 8
ITERS = 3
step_eta = 0.4
low_density = 0.35
high_density = 0.65
layer_gap = 0.15
tiny_term = 1e-06


def extended(cells, sides, width):
    for axis, dim in sides:
        count = lax.axis_size(axis)
        ends = count - 1
        head = lax.slice_in_dim(cells, 0, width, axis=dim)
        tail = lax.slice_in_dim(cells, cells.shape[dim] - width, cells.shape[dim], axis=dim)
        cells = jnp.concatenate(
            [
                lax.ppermute(tail, axis, [(i, (i + 1) % count) for i in range(ends)]),
                cells,
                lax.ppermute(head, axis, [((i + 1) % count, i) for i in range(ends)]),
            ],
            axis=dim,
        )
    return cells


def from_behind(block, axis, distance):
    devices = range(lax.axis_size(axis))
    route = [(i - distance, i) for i in devices if i - distance in devices]
    return lax.ppermute(block, axis, route)


def band_matrix(extent_out, extent_in, offset):
    index_out = lax.broadcasted_iota(jnp.int32, (extent_out, extent_in), 0)
    index_in = lax.broadcasted_iota(jnp.int32, (extent_out, extent_in), 1)
    spread = index_in - index_out
    return ((spread >= offset) & (spread < offset + WIN)).astype(jnp.float32)


def rows_pass(row_band, padded):
    return jnp.einsum("ip,lpq->liq", row_band, padded, precision=lax.Precision.HIGHEST)


def cols_pass(partial_sum, col_band):
    return jnp.einsum("liq,qj->lij", partial_sum, col_band, precision=lax.Precision.HIGHEST)


def fill_window(level, row_band, col_band, halfway):
    tall = extended(level, (("row", 1),), halfway)
    partial_sum = rows_pass(row_band, tall)
    wide = extended(partial_sum, (("col", 2),), halfway)
    result = cols_pass(wide, col_band)
    return result


def dual_window(density_dual, row_band, col_band, halfway):
    tall = extended(density_dual, (("row", 1),), halfway)
    partial_sum = rows_pass(row_band, tall)
    wide = extended(partial_sum, (("col", 2),), halfway)
    result = cols_pass(wide, col_band)
    return result


def local(cost_vector, metal_density, cap_class, blocked_mask, fill_start, window_dual, layer_dual):
    layers_here, row_count, col_count = fill_start.shape
    halfway = WIN // 2
    inverse_area = 1.0 / (WIN * WIN)
    row_forward = band_matrix(row_count, row_count + 2 * halfway, 0)
    row_backward = band_matrix(row_count, row_count + 2 * halfway, 1)
    col_forward = band_matrix(col_count, col_count + 2 * halfway, 0).T
    col_backward = band_matrix(col_count, col_count + 2 * halfway, 1).T
    layer_ids = lax.axis_index("layer") * layers_here + lax.iota(jnp.int32, layers_here)
    keep_mask = (layer_ids < lax.axis_size("layer") * layers_here - 1).astype(jnp.float32)[
        :, None, None
    ]
    capacity = jnp.where(blocked_mask == 1, 0.0, (cap_class + 1).astype(jnp.float32) / CAP_LEVELS)
    has_floor = blocked_mask == 0
    filling = fill_start
    density_dual = window_dual
    stacked_dual = layer_dual * keep_mask
    weight = jnp.float32(1.0)
    for iteration in range(ITERS):
        primal_step = step_eta / weight
        dual_step = step_eta * weight
        below = from_behind(stacked_dual[layers_here - 1 :], "layer", 1)
        earlier = jnp.concatenate([below, stacked_dual[: layers_here - 1]], axis=0)
        transposed = dual_window(density_dual, row_backward, col_backward, halfway)
        gradient = cost_vector + transposed * inverse_area + (stacked_dual - earlier)
        fill_new = jnp.clip(filling - primal_step * gradient, 0.0, capacity)
        moved = fill_new - filling
        primal_sum = jnp.sum(moved * moved)
        level = fill_new + moved + metal_density
        above = from_behind(level[0:1], "layer", -1)
        later = jnp.concatenate([level[1:], above], axis=0)
        forward = fill_window(level, row_forward, col_forward, halfway)
        window_term = density_dual / dual_step + forward * inverse_area
        capped = jnp.minimum(window_term, high_density)
        clipped = jnp.where(has_floor, jnp.maximum(capped, low_density), capped)
        density_new = dual_step * (window_term - clipped)
        layer_term = stacked_dual / dual_step + keep_mask * (level - later)
        stacked_new = (
            dual_step * (layer_term - jnp.clip(layer_term, -layer_gap, layer_gap)) * keep_mask
        )
        density_move = density_new - density_dual
        stacked_move = stacked_new - stacked_dual
        dual_sum = jnp.sum(density_move * density_move) + jnp.sum(stacked_move * stacked_move)
        primal_sum, dual_sum = lax.psum((primal_sum, dual_sum), ("layer", "row", "col"))
        weight = jnp.sqrt(weight) * jnp.sqrt(
            jnp.sqrt((dual_sum + tiny_term) / (primal_sum + tiny_term))
        )
        filling = fill_new
        density_dual = density_new
        stacked_dual = stacked_new
    return (filling, density_dual, stacked_dual, weight)


def solution(mesh):
    in_specs = (
        P("layer", "row", "col"),
        P("layer", "row", "col"),
        P("layer", "row", "col"),
        P("layer", "row", "col"),
        P("layer", "row", "col"),
        P("layer", "row", "col"),
        P("layer", "row", "col"),
    )
    out_specs = (P("layer", "row", "col"), P("layer", "row", "col"), P("layer", "row", "col"), P())
    return jax.shard_map(local, mesh=mesh, in_specs=in_specs, out_specs=out_specs, check_vma=False)
```

profile of v0, /device:TPU:0, one launch (start us, length us, event | category | flops | bytes accessed | tf_op | source)
XLA Modules:
  0.0 268.0 jit_solution(12571616555059935040)
XLA Ops:
  1.4 4.9 %collective-permute-start = (f32[2,25,128]{2,1,0:T(8,128)S(1)}, f32[2,25,128]{2,1,0:T(8,128)S(1)}, u32[]{:S(2)}, u32[]{:S(2)}) collective-permute-start(f32[2,25,128]{2,1,0:T(8,128)S(1)} %get-tuple-element.56), channel_id=1, source_target_pairs={{0,4},{1,5},{2,6},{3,7},{8,12},{9,13},{10,14},{11,15},{16,20},{17,... | collective-permute-start | bytes 76808 | tf_op jit(solution)/shard_map/ppermute | solution.py:24
  8.8 3.6 %collective-permute-start.4 = (f32[1,512,128]{2,1,0:T(8,128)S(1)}, f32[1,512,128]{2,1,0:T(8,128)S(1)}, u32[]{:S(2)}, u32[]{:S(2)}) collective-permute-start(f32[1,512,128]{2,1,0:T(8,128)S(1)} %get-tuple-element.52), channel_id=1, source_target_pairs={{0,8},{8,16},{16,24},{1,9},{9,17},{17,25},{2,10},{10,18},{18,26},{... | collective-permute-start | bytes 786440 | tf_op jit(solution)/shard_map/ppermute | solution.py:36
  16.2 3.7 %collective-permute-done.3 = f32[2,512,25]{1,2,0:T(8,128)S(1)} collective-permute-done((f32[2,512,25]{1,2,0:T(8,128)S(1)}, f32[2,512,25]{1,2,0:T(8,128)S(1)}, u32[]{:S(2)}, u32[]{:S(2)}) %collective-permute-start.3) | collective-permute-done | bytes 102432 | tf_op jit(solution)/shard_map/ppermute | solution.py:26
  20.0 2.5 multiply_reduce_fusion.6
  22.5 4.5 %collective-permute-start.5 = (f32[2,25,128]{2,1,0:T(8,128)S(1)}, f32[2,25,128]{2,1,0:T(8,128)S(1)}, u32[]{:S(2)}, u32[]{:S(2)}) collective-permute-start(f32[2,25,128]{2,1,0:T(8,128)S(1)} %get-tuple-element.50), channel_id=1, source_target_pairs={{0,4},{1,5},{2,6},{3,7},{8,12},{9,13},{10,14},{11,15},{16,20},{17,... | collective-permute-start | bytes 76808 | tf_op jit(solution)/shard_map/ppermute | solution.py:24
  28.6 4.2 %collective-permute-done.6 = f32[2,25,128]{2,1,0:T(8,128)S(1)} collective-permute-done((f32[2,25,128]{2,1,0:T(8,128)S(1)}, f32[2,25,128]{2,1,0:T(8,128)S(1)}, u32[]{:S(2)}, u32[]{:S(2)}) %collective-permute-start.6) | collective-permute-done | bytes 25632 | tf_op jit(solution)/shard_map/ppermute | solution.py:26
  33.8 4.0 %collective-permute-start.7 = (f32[2,512,25]{1,2,0:T(8,128)S(1)}, f32[2,512,25]{1,2,0:T(8,128)S(1)}, u32[]{:S(2)}, u32[]{:S(2)}) collective-permute-start(f32[2,512,25]{1,2,0:T(8,128)S(1)} %get-tuple-element.48), channel_id=1, source_target_pairs={{0,1},{1,2},{2,3},{4,5},{5,6},{6,7},{8,9},{9,10},{10,11},{12,13},{... | collective-permute-start | bytes 307208 | tf_op jit(solution)/shard_map/ppermute | solution.py:24
  46.8 4.2 %collective-permute-done.11 = f32[2,25,128]{2,1,0:T(8,128)S(1)} collective-permute-done((f32[2,25,128]{2,1,0:T(8,128)S(1)}, f32[2,25,128]{2,1,0:T(8,128)S(1)}, u32[]{:S(2)}, u32[]{:S(2)}) %collective-permute-start.11) | collective-permute-done | bytes 25632 | tf_op jit(solution)/shard_map/ppermute | solution.py:26
  52.9 3.5 %collective-permute-start.14 = (f32[1,512,128]{2,1,0:T(8,128)S(1)}, f32[1,512,128]{2,1,0:T(8,128)S(1)}, u32[]{:S(2)}, u32[]{:S(2)}) collective-permute-start(f32[1,512,128]{2,1,0:T(8,128)S(1)} %get-tuple-element.40), channel_id=1, source_target_pairs={{0,8},{8,16},{16,24},{1,9},{9,17},{17,25},{2,10},{10,18},{18,26},{... | collective-permute-start | bytes 786440 | tf_op jit(solution)/shard_map/ppermute | solution.py:36
  57.2 4.7 %collective-permute-start.12 = (f32[2,512,25]{1,2,0:T(8,128)}, f32[2,512,25]{1,2,0:T(8,128)}, u32[]{:S(2)}, u32[]{:S(2)}) collective-permute-start(f32[2,512,25]{1,2,0:T(8,128)} %get-tuple-element.44), channel_id=1, source_target_pairs={{0,1},{1,2},{2,3},{4,5},{5,6},{6,7},{8,9},{9,10},{10,11},{12,13},{... | collective-permute-start | bytes 307208 | tf_op jit(solution)/shard_map/ppermute | solution.py:24
  64.4 40.6 %all-reduce.2 = (f32[]{:T(128)}, f32[]{:T(128)}) all-reduce(f32[]{:T(128)S(6)} %add.115, f32[]{:T(128)} %get-tuple-element.20), channel_id=1, replica_groups=mesh['layer'=4,'row'=2,'col'=4] {'layer','row','col'}, use_global_device_ids=true, to_apply=%region_2.3 | all-reduce | flops 2 | bytes 16 | tf_op jit(solution)/shard_map/psum | solution.py:113
  107.2 3.9 %multiply_reduce_fusion.3 = (f32[]{:T(128)}, f32[2,512,128]{2,1,0:T(8,128)S(1)}, f32[2,512,128]{2,1,0:T(8,128)}) fusion(f32[2,512,128]{2,1,0:T(8,128)} %get-tuple-element.58, f32[2,512,128]{2,1,0:T(8,128)S(1)} %copy-done.1, f32[2,512,128]{2,1,0:T(8,128)S(1)} %get-tuple-element.15, f32[1,512,128]{2,1,0:T(8,128)S(1)} %get-tuple-element.41, ...), kind=kOutput, calls=%fused_computation.139 | convolution fusion | flops 282915840 | bytes 5447688 | tf_op jit(solution)/shard_map/liq,qj->lij/dot_general | solution.py:51
  111.1 4.2 %collective-permute-start.15 = (f32[2,25,128]{2,1,0:T(8,128)S(1)}, f32[2,25,128]{2,1,0:T(8,128)S(1)}, u32[]{:S(2)}, u32[]{:S(2)}) collective-permute-start(f32[2,25,128]{2,1,0:T(8,128)S(1)} %get-tuple-element.38), channel_id=1, source_target_pairs={{0,4},{1,5},{2,6},{3,7},{8,12},{9,13},{10,14},{11,15},{16,20},{17,... | collective-permute-start | bytes 76808 | tf_op jit(solution)/shard_map/ppermute | solution.py:24
  116.8 4.2 %collective-permute-done.16 = f32[2,25,128]{2,1,0:T(8,128)S(1)} collective-permute-done((f32[2,25,128]{2,1,0:T(8,128)S(1)}, f32[2,25,128]{2,1,0:T(8,128)S(1)}, u32[]{:S(2)}, u32[]{:S(2)}) %collective-permute-start.16) | collective-permute-done | bytes 25632 | tf_op jit(solution)/shard_map/ppermute | solution.py:26
  126.1 2.9 %collective-permute-done.18 = f32[2,512,25]{1,2,0:T(8,128)S(1)} collective-permute-done((f32[2,512,25]{1,2,0:T(8,128)S(1)}, f32[2,512,25]{1,2,0:T(8,128)S(1)}, u32[]{:S(2)}, u32[]{:S(2)}) %collective-permute-start.18) | collective-permute-done | bytes 102432 | tf_op jit(solution)/shard_map/ppermute | solution.py:26
  134.0 4.2 %collective-permute-done.21 = f32[2,25,128]{2,1,0:T(8,128)S(1)} collective-permute-done((f32[2,25,128]{2,1,0:T(8,128)S(1)}, f32[2,25,128]{2,1,0:T(8,128)S(1)}, u32[]{:S(2)}, u32[]{:S(2)}) %collective-permute-start.21) | collective-permute-done | bytes 25632 | tf_op jit(solution)/shard_map/ppermute | solution.py:26
  143.3 4.7 %collective-permute-start.22 = (f32[2,512,25]{1,2,0:T(8,128)}, f32[2,512,25]{1,2,0:T(8,128)}, u32[]{:S(2)}, u32[]{:S(2)}) collective-permute-start(f32[2,512,25]{1,2,0:T(8,128)} %get-tuple-element.32), channel_id=1, source_target_pairs={{0,1},{1,2},{2,3},{4,5},{5,6},{6,7},{8,9},{9,10},{10,11},{12,13},{... | collective-permute-start | bytes 307208 | tf_op jit(solution)/shard_map/ppermute | solution.py:24
  150.6 40.6 %all-reduce.1 = (f32[]{:T(128)}, f32[]{:T(128)}) all-reduce(f32[]{:T(128)S(6)} %add.124, f32[]{:T(128)} %get-tuple-element.18), channel_id=1, replica_groups=mesh['layer'=4,'row'=2,'col'=4] {'layer','row','col'}, use_global_device_ids=true, to_apply=%region_7.8 | all-reduce | flops 2 | bytes 16 | tf_op jit(solution)/shard_map/psum | solution.py:113
  193.4 3.9 %multiply_reduce_fusion = (f32[]{:T(128)}, f32[2,512,128]{2,1,0:T(8,128)S(1)}, f32[2,512,128]{2,1,0:T(8,128)}) fusion(f32[2,512,128]{2,1,0:T(8,128)} %get-tuple-element.61, f32[2,512,128]{2,1,0:T(8,128)S(1)} %copy-done.1, f32[2,512,128]{2,1,0:T(8,128)S(1)} %get-tuple-element.13, f32[1,512,128]{2,1,0:T(8,128)S(1)} %get-tuple-element.29, ...), kind=kOutput, calls=%fused_computation.134 | convolution fusion | flops 282915840 | bytes 5447688 | tf_op jit(solution)/shard_map/liq,qj->lij/dot_general | solution.py:51
  197.3 4.2 %collective-permute-start.25 = (f32[2,25,128]{2,1,0:T(8,128)S(1)}, f32[2,25,128]{2,1,0:T(8,128)S(1)}, u32[]{:S(2)}, u32[]{:S(2)}) collective-permute-start(f32[2,25,128]{2,1,0:T(8,128)S(1)} %get-tuple-element.26), channel_id=1, source_target_pairs={{0,4},{1,5},{2,6},{3,7},{8,12},{9,13},{10,14},{11,15},{16,20},{17,... | collective-permute-start | bytes 76808 | tf_op jit(solution)/shard_map/ppermute | solution.py:24
  203.1 4.2 %collective-permute-done.26 = f32[2,25,128]{2,1,0:T(8,128)S(1)} collective-permute-done((f32[2,25,128]{2,1,0:T(8,128)S(1)}, f32[2,25,128]{2,1,0:T(8,128)S(1)}, u32[]{:S(2)}, u32[]{:S(2)}) %collective-permute-start.26) | collective-permute-done | bytes 25632 | tf_op jit(solution)/shard_map/ppermute | solution.py:26
  212.4 2.9 %collective-permute-done.28 = f32[2,512,25]{1,2,0:T(8,128)S(1)} collective-permute-done((f32[2,512,25]{1,2,0:T(8,128)S(1)}, f32[2,512,25]{1,2,0:T(8,128)S(1)}, u32[]{:S(2)}, u32[]{:S(2)}) %collective-permute-start.28) | collective-permute-done | bytes 102432 | tf_op jit(solution)/shard_map/ppermute | solution.py:26
  215.3 2.5 multiply_reduce_fusion.2
  222.5 43.0 %all-reduce = (f32[]{:T(128)}, f32[]{:T(128)}) all-reduce(f32[]{:T(128)S(6)} %add.133, f32[]{:T(128)} %get-tuple-element.16), channel_id=1, replica_groups=mesh['layer'=4,'row'=2,'col'=4] {'layer','row','col'}, use_global_device_ids=true, to_apply=%region_12.13 | all-reduce | flops 2 | bytes 16 | tf_op jit(solution)/shard_map/psum | solution.py:113
  (108 shorter events, 51.4 us)
Async XLA Ops:
  1.4 11.0 %collective-permute-start = (f32[2,25,128]{2,1,0:T(8,128)S(1)}, f32[2,25,128]{2,1,0:T(8,128)S(1)}, u32[]{:S(2)}, u32[]{:S(2)}) collective-permute-start(f32[2,25,128]{2,1,0:T(8,128)S(1)} %get-tuple-element.56), channel_id=1, source_target_pairs={{0,4},{1,5},{2,6},{3,7},{8,12},{9,13},{10,14},{11,15},{16,20},{17,... | collective-permute-start | bytes 76808 | tf_op jit(solution)/shard_map/ppermute | solution.py:24
  6.3 6.2 %collective-permute-start.1 = (f32[2,25,128]{2,1,0:T(8,128)S(1)}, f32[2,25,128]{2,1,0:T(8,128)S(1)}, u32[]{:S(2)}, u32[]{:S(2)}) collective-permute-start(f32[2,25,128]{2,1,0:T(8,128)S(1)} %get-tuple-element.57), channel_id=1, source_target_pairs={{4,0},{5,1},{6,2},{7,3},{12,8},{13,9},{14,10},{15,11},{20,16},{21,... | collective-permute-start | bytes 76808 | tf_op jit(solution)/shard_map/ppermute | solution.py:26
  8.8 11.1 %collective-permute-start.4 = (f32[1,512,128]{2,1,0:T(8,128)S(1)}, f32[1,512,128]{2,1,0:T(8,128)S(1)}, u32[]{:S(2)}, u32[]{:S(2)}) collective-permute-start(f32[1,512,128]{2,1,0:T(8,128)S(1)} %get-tuple-element.52), channel_id=1, source_target_pairs={{0,8},{8,16},{16,24},{1,9},{9,17},{17,25},{2,10},{10,18},{18,26},{... | collective-permute-start | bytes 786440 | tf_op jit(solution)/shard_map/ppermute | solution.py:36
  14.9 5.0 %collective-permute-start.3 = (f32[2,512,25]{1,2,0:T(8,128)S(1)}, f32[2,512,25]{1,2,0:T(8,128)S(1)}, u32[]{:S(2)}, u32[]{:S(2)}) collective-permute-start(f32[2,512,25]{1,2,0:T(8,128)S(1)} %get-tuple-element.55), channel_id=1, source_target_pairs={{1,0},{2,1},{3,2},{5,4},{6,5},{7,6},{9,8},{10,9},{11,10},{13,12},{... | collective-permute-start | bytes 307208 | tf_op jit(solution)/shard_map/ppermute | solution.py:26
  22.5 6.1 %collective-permute-start.5 = (f32[2,25,128]{2,1,0:T(8,128)S(1)}, f32[2,25,128]{2,1,0:T(8,128)S(1)}, u32[]{:S(2)}, u32[]{:S(2)}) collective-permute-start(f32[2,25,128]{2,1,0:T(8,128)S(1)} %get-tuple-element.50), channel_id=1, source_target_pairs={{0,4},{1,5},{2,6},{3,7},{8,12},{9,13},{10,14},{11,15},{16,20},{17,... | collective-permute-start | bytes 76808 | tf_op jit(solution)/shard_map/ppermute | solution.py:24
  27.0 5.8 %collective-permute-start.6 = (f32[2,25,128]{2,1,0:T(8,128)S(1)}, f32[2,25,128]{2,1,0:T(8,128)S(1)}, u32[]{:S(2)}, u32[]{:S(2)}) collective-permute-start(f32[2,25,128]{2,1,0:T(8,128)S(1)} %get-tuple-element.51), channel_id=1, source_target_pairs={{4,0},{5,1},{6,2},{7,3},{12,8},{13,9},{14,10},{15,11},{20,16},{21,... | collective-permute-start | bytes 76808 | tf_op jit(solution)/shard_map/ppermute | solution.py:26
  33.8 6.7 %collective-permute-start.7 = (f32[2,512,25]{1,2,0:T(8,128)S(1)}, f32[2,512,25]{1,2,0:T(8,128)S(1)}, u32[]{:S(2)}, u32[]{:S(2)}) collective-permute-start(f32[2,512,25]{1,2,0:T(8,128)S(1)} %get-tuple-element.48), channel_id=1, source_target_pairs={{0,1},{1,2},{2,3},{4,5},{5,6},{6,7},{8,9},{9,10},{10,11},{12,13},{... | collective-permute-start | bytes 307208 | tf_op jit(solution)/shard_map/ppermute | solution.py:24
  39.2 12.8 %collective-permute-start.9 = (f32[1,512,128]{2,1,0:T(8,128)S(1)}, f32[1,512,128]{2,1,0:T(8,128)S(1)}, u32[]{:S(2)}, u32[]{:S(2)}) collective-permute-start(f32[1,512,128]{2,1,0:T(8,128)S(1)} %get-tuple-element.43), channel_id=1, source_target_pairs={{8,0},{16,8},{24,16},{9,1},{17,9},{25,17},{10,2},{18,10},{26,18},{... | collective-permute-start | bytes 786440 | tf_op jit(solution)/shard_map/ppermute | solution.py:36
  45.2 5.8 %collective-permute-start.11 = (f32[2,25,128]{2,1,0:T(8,128)S(1)}, f32[2,25,128]{2,1,0:T(8,128)S(1)}, u32[]{:S(2)}, u32[]{:S(2)}) collective-permute-start(f32[2,25,128]{2,1,0:T(8,128)S(1)} %get-tuple-element.47), channel_id=1, source_target_pairs={{4,0},{5,1},{6,2},{7,3},{12,8},{13,9},{14,10},{15,11},{20,16},{21,... | collective-permute-start | bytes 76808 | tf_op jit(solution)/shard_map/ppermute | solution.py:26
  52.9 53.5 %collective-permute-start.14 = (f32[1,512,128]{2,1,0:T(8,128)S(1)}, f32[1,512,128]{2,1,0:T(8,128)S(1)}, u32[]{:S(2)}, u32[]{:S(2)}) collective-permute-start(f32[1,512,128]{2,1,0:T(8,128)S(1)} %get-tuple-element.40), channel_id=1, source_target_pairs={{0,8},{8,16},{16,24},{1,9},{9,17},{17,25},{2,10},{10,18},{18,26},{... | collective-permute-start | bytes 786440 | tf_op jit(solution)/shard_map/ppermute | solution.py:36
  57.2 49.2 %collective-permute-start.12 = (f32[2,512,25]{1,2,0:T(8,128)}, f32[2,512,25]{1,2,0:T(8,128)}, u32[]{:S(2)}, u32[]{:S(2)}) collective-permute-start(f32[2,512,25]{1,2,0:T(8,128)} %get-tuple-element.44), channel_id=1, source_target_pairs={{0,1},{1,2},{2,3},{4,5},{5,6},{6,7},{8,9},{9,10},{10,11},{12,13},{... | collective-permute-start | bytes 307208 | tf_op jit(solution)/shard_map/ppermute | solution.py:24
  61.9 44.6 %collective-permute-start.13 = (f32[2,512,25]{1,2,0:T(8,128)}, f32[2,512,25]{1,2,0:T(8,128)}, u32[]{:S(2)}, u32[]{:S(2)}) collective-permute-start(f32[2,512,25]{1,2,0:T(8,128)} %get-tuple-element.45), channel_id=1, source_target_pairs={{1,0},{2,1},{3,2},{5,4},{6,5},{7,6},{9,8},{10,9},{11,10},{13,12},{... | collective-permute-start | bytes 307208 | tf_op jit(solution)/shard_map/ppermute | solution.py:26
  111.1 5.8 %collective-permute-start.15 = (f32[2,25,128]{2,1,0:T(8,128)S(1)}, f32[2,25,128]{2,1,0:T(8,128)S(1)}, u32[]{:S(2)}, u32[]{:S(2)}) collective-permute-start(f32[2,25,128]{2,1,0:T(8,128)S(1)} %get-tuple-element.38), channel_id=1, source_target_pairs={{0,4},{1,5},{2,6},{3,7},{8,12},{9,13},{10,14},{11,15},{16,20},{17,... | collective-permute-start | bytes 76808 | tf_op jit(solution)/shard_map/ppermute | solution.py:24
  115.2 5.8 %collective-permute-start.16 = (f32[2,25,128]{2,1,0:T(8,128)S(1)}, f32[2,25,128]{2,1,0:T(8,128)S(1)}, u32[]{:S(2)}, u32[]{:S(2)}) collective-permute-start(f32[2,25,128]{2,1,0:T(8,128)S(1)} %get-tuple-element.39), channel_id=1, source_target_pairs={{4,0},{5,1},{6,2},{7,3},{12,8},{13,9},{14,10},{15,11},{20,16},{21,... | collective-permute-start | bytes 76808 | tf_op jit(solution)/shard_map/ppermute | solution.py:26
  123.3 5.7 %collective-permute-start.18 = (f32[2,512,25]{1,2,0:T(8,128)S(1)}, f32[2,512,25]{1,2,0:T(8,128)S(1)}, u32[]{:S(2)}, u32[]{:S(2)}) collective-permute-start(f32[2,512,25]{1,2,0:T(8,128)S(1)} %get-tuple-element.37), channel_id=1, source_target_pairs={{1,0},{2,1},{3,2},{5,4},{6,5},{7,6},{9,8},{10,9},{11,10},{13,12},{... | collective-permute-start | bytes 307208 | tf_op jit(solution)/shard_map/ppermute | solution.py:26
  124.8 14.4 %collective-permute-start.19 = (f32[1,512,128]{2,1,0:T(8,128)S(1)}, f32[1,512,128]{2,1,0:T(8,128)S(1)}, u32[]{:S(2)}, u32[]{:S(2)}) collective-permute-start(f32[1,512,128]{2,1,0:T(8,128)S(1)} %get-tuple-element.31), channel_id=1, source_target_pairs={{8,0},{16,8},{24,16},{9,1},{17,9},{25,17},{10,2},{18,10},{26,18},{... | collective-permute-start | bytes 786440 | tf_op jit(solution)/shard_map/ppermute | solution.py:36
  132.4 5.8 %collective-permute-start.21 = (f32[2,25,128]{2,1,0:T(8,128)S(1)}, f32[2,25,128]{2,1,0:T(8,128)S(1)}, u32[]{:S(2)}, u32[]{:S(2)}) collective-permute-start(f32[2,25,128]{2,1,0:T(8,128)S(1)} %get-tuple-element.35), channel_id=1, source_target_pairs={{4,0},{5,1},{6,2},{7,3},{12,8},{13,9},{14,10},{15,11},{20,16},{21,... | collective-permute-start | bytes 76808 | tf_op jit(solution)/shard_map/ppermute | solution.py:26
  140.2 52.5 %collective-permute-start.24 = (f32[1,512,128]{2,1,0:T(8,128)S(1)}, f32[1,512,128]{2,1,0:T(8,128)S(1)}, u32[]{:S(2)}, u32[]{:S(2)}) collective-permute-start(f32[1,512,128]{2,1,0:T(8,128)S(1)} %get-tuple-element.28), channel_id=1, source_target_pairs={{0,8},{8,16},{16,24},{1,9},{9,17},{17,25},{2,10},{10,18},{18,26},{... | collective-permute-start | bytes 786440 | tf_op jit(solution)/shard_map/ppermute | solution.py:36
  143.3 49.4 %collective-permute-start.22 = (f32[2,512,25]{1,2,0:T(8,128)}, f32[2,512,25]{1,2,0:T(8,128)}, u32[]{:S(2)}, u32[]{:S(2)}) collective-permute-start(f32[2,512,25]{1,2,0:T(8,128)} %get-tuple-element.32), channel_id=1, source_target_pairs={{0,1},{1,2},{2,3},{4,5},{5,6},{6,7},{8,9},{9,10},{10,11},{12,13},{... | collective-permute-start | bytes 307208 | tf_op jit(solution)/shard_map/ppermute | solution.py:24
  148.0 44.7 %collective-permute-start.23 = (f32[2,512,25]{1,2,0:T(8,128)}, f32[2,512,25]{1,2,0:T(8,128)}, u32[]{:S(2)}, u32[]{:S(2)}) collective-permute-start(f32[2,512,25]{1,2,0:T(8,128)} %get-tuple-element.33), channel_id=1, source_target_pairs={{1,0},{2,1},{3,2},{5,4},{6,5},{7,6},{9,8},{10,9},{11,10},{13,12},{... | collective-permute-start | bytes 307208 | tf_op jit(solution)/shard_map/ppermute | solution.py:26
  197.3 5.8 %collective-permute-start.25 = (f32[2,25,128]{2,1,0:T(8,128)S(1)}, f32[2,25,128]{2,1,0:T(8,128)S(1)}, u32[]{:S(2)}, u32[]{:S(2)}) collective-permute-start(f32[2,25,128]{2,1,0:T(8,128)S(1)} %get-tuple-element.26), channel_id=1, source_target_pairs={{0,4},{1,5},{2,6},{3,7},{8,12},{9,13},{10,14},{11,15},{16,20},{17,... | collective-permute-start | bytes 76808 | tf_op jit(solution)/shard_map/ppermute | solution.py:24
  201.5 5.8 %collective-permute-start.26 = (f32[2,25,128]{2,1,0:T(8,128)S(1)}, f32[2,25,128]{2,1,0:T(8,128)S(1)}, u32[]{:S(2)}, u32[]{:S(2)}) collective-permute-start(f32[2,25,128]{2,1,0:T(8,128)S(1)} %get-tuple-element.27), channel_id=1, source_target_pairs={{4,0},{5,1},{6,2},{7,3},{12,8},{13,9},{14,10},{15,11},{20,16},{21,... | collective-permute-start | bytes 76808 | tf_op jit(solution)/shard_map/ppermute | solution.py:26
  209.5 5.7 %collective-permute-start.28 = (f32[2,512,25]{1,2,0:T(8,128)S(1)}, f32[2,512,25]{1,2,0:T(8,128)S(1)}, u32[]{:S(2)}, u32[]{:S(2)}) collective-permute-start(f32[2,512,25]{1,2,0:T(8,128)S(1)} %get-tuple-element.25), channel_id=1, source_target_pairs={{1,0},{2,1},{3,2},{5,4},{6,5},{7,6},{9,8},{10,9},{11,10},{13,12},{... | collective-permute-start | bytes 307208 | tf_op jit(solution)/shard_map/ppermute | solution.py:26
  211.0 8.6 %collective-permute-start.29 = (f32[1,512,128]{2,1,0:T(8,128)S(1)}, f32[1,512,128]{2,1,0:T(8,128)S(1)}, u32[]{:S(2)}, u32[]{:S(2)}) collective-permute-start(f32[1,512,128]{2,1,0:T(8,128)S(1)} %get-tuple-element.23), channel_id=1, source_target_pairs={{8,0},{16,8},{24,16},{9,1},{17,9},{25,17},{10,2},{18,10},{26,18},{... | collective-permute-start | bytes 786440 | tf_op jit(solution)/shard_map/ppermute | solution.py:36
  (22 other events, 157.5 us)
where the time goes:
time: 269 us; the launch traced here: 268 us
  blocking collectives  124 us (46%)
  starting transfers between devices  67.7 us (25%)
  waiting for transfers between devices  35 us (13%)
  matrix products  21.7 us (8%)
  between operations  10.6 us (4%)
  other arithmetic  4.76 us (2%)
  local copies, waits for them, and re-layouts  4.08 us (2%)
    psum x3, blocking collectives, local(): lax.psum((primal_sum, dual_sum), ('layer', 'row', 'col'))  124 us
    ppermute x12, starting transfers between devices, extended(): lax.ppermute(tail, axis, [(i, (i + 1) % count) for i in range(ends)])  38.4 us
    ppermute x12, waiting for transfers between devices, extended(): lax.ppermute(head, axis, [((i + 1) % count, i) for i in range(ends)])  32.1 us
    dot_general x6, matrix products, cols_pass(): jnp.einsum('liq,qj->lij', partial_sum, col_band, precision=lax.Precision....  16.3 us
    ppermute x12, starting transfers between devices, extended(): lax.ppermute(head, axis, [((i + 1) % count, i) for i in range(ends)])  15.9 us
    ppermute x6, starting transfers between devices, from_behind(): return lax.ppermute(block, axis, route)  13.4 us
    dot_general x6, matrix products, rows_pass(): jnp.einsum('ip,lpq->liq', row_band, padded, precision=lax.Precision.HIGHEST)  5.39 us
  transfers between devices with their start and end apart: 30, of which 15 were waited for; matrix products, arithmetic and copies ran while one was open for 4% of the time, Pallas kernels for 0%

commit v1 on v0

--- a/solution.py
+++ b/solution.py
@@ -110,7 +110,7 @@
         density_move = density_new - density_dual
         stacked_move = stacked_new - stacked_dual
         dual_sum = jnp.sum(density_move * density_move) + jnp.sum(stacked_move * stacked_move)
-        primal_sum, dual_sum = lax.psum((primal_sum, dual_sum), ("layer", "row", "col"))
+        primal_sum, dual_sum = lax.psum(lax.psum((primal_sum, dual_sum), ("row", "col")), "layer")
         weight = jnp.sqrt(weight) * jnp.sqrt(
             jnp.sqrt((dual_sum + tiny_term) / (primal_sum + tiny_term))
         )

time: 269 us -> 215 us (0.80)
  blocking collectives: 124 us -> 71.2 us
    psum x3 -> x6, blocking collectives: 124 us -> 71.2 us  [the longest x3 40.8 us: local(): lax.psum((primal_sum, dual_sum), ('row', 'col'))]
    ppermute x6, waiting for transfers between devices: 1.77 us -> 6.5 us  [from_behind(): return lax.ppermute(block, axis, route)]
    ppermute x12, waiting for transfers between devices: 32.1 us -> 27.3 us  [extended(): lax.ppermute(head, axis, [((i + 1) % count, i) for i in range(ends)])]
    ppermute x12, starting transfers between devices: 38.4 us -> 35.6 us  [extended(): lax.ppermute(tail, axis, [(i, (i + 1) % count) for i in range(ends)])]
  transfers between devices with their start and end apart: 30 -> 30, of which waited for: 15 -> 15; matrix products, arithmetic and copies ran while one was open for 4% -> 5% of each run, Pallas kernels for 0% -> 0%
where the time goes in v1:
time: 215 us; the launch traced here: 214 us
  blocking collectives  71.2 us (33%)
  starting transfers between devices  66.9 us (31%)
  waiting for transfers between devices  35 us (16%)
  matrix products  21.7 us (10%)
  between operations  10.2 us (5%)
  other arithmetic  4.7 us (2%)
  local copies, waits for them, and re-layouts  4.03 us (2%)
    psum x3, blocking collectives, local(): lax.psum((primal_sum, dual_sum), ('row', 'col'))  40.8 us
    ppermute x12, starting transfers between devices, extended(): lax.ppermute(tail, axis, [(i, (i + 1) % count) for i in range(ends)])  35.6 us
    psum x3, blocking collectives, local(): lax.psum(lax.psum((primal_sum, dual_sum), ('row', 'col')), 'layer')  30.4 us
    ppermute x12, waiting for transfers between devices, extended(): lax.ppermute(head, axis, [((i + 1) % count, i) for i in range(ends)])  27.3 us
    dot_general x6, matrix products, cols_pass(): jnp.einsum('liq,qj->lij', partial_sum, col_band, precision=lax.Precision....  16.3 us
    ppermute x12, starting transfers between devices, extended(): lax.ppermute(head, axis, [((i + 1) % count, i) for i in range(ends)])  15.9 us
    ppermute x6, starting transfers between devices, from_behind(): return lax.ppermute(block, axis, route)  15.4 us
    ppermute x6, waiting for transfers between devices, from_behind(): return lax.ppermute(block, axis, route)  6.5 us
  transfers between devices with their start and end apart: 30, of which 15 were waited for; matrix products, arithmetic and copies ran while one was open for 5% of the time, Pallas kernels for 0%

profile of v1, /device:TPU:0, one launch (start us, length us, event | category | flops | bytes accessed | tf_op | source)
XLA Modules:
  0.0 213.8 jit_solution(9699976677255762976)
XLA Ops:
  1.4 4.9 %collective-permute-start = (f32[2,25,128]{2,1,0:T(8,128)S(1)}, f32[2,25,128]{2,1,0:T(8,128)S(1)}, u32[]{:S(2)}, u32[]{:S(2)}) collective-permute-start(f32[2,25,128]{2,1,0:T(8,128)S(1)} %get-tuple-element.62), channel_id=1, source_target_pairs={{0,4},{1,5},{2,6},{3,7},{8,12},{9,13},{10,14},{11,15},{16,20},{17,... | collective-permute-start | bytes 76808 | tf_op jit(solution)/shard_map/ppermute | solution.py:24
  8.8 3.6 %collective-permute-start.4 = (f32[1,512,128]{2,1,0:T(8,128)S(1)}, f32[1,512,128]{2,1,0:T(8,128)S(1)}, u32[]{:S(2)}, u32[]{:S(2)}) collective-permute-start(f32[1,512,128]{2,1,0:T(8,128)S(1)} %get-tuple-element.58), channel_id=1, source_target_pairs={{0,8},{8,16},{16,24},{1,9},{9,17},{17,25},{2,10},{10,18},{18,26},{... | collective-permute-start | bytes 786440 | tf_op jit(solution)/shard_map/ppermute | solution.py:36
  16.2 3.7 %collective-permute-done.3 = f32[2,512,25]{1,2,0:T(8,128)S(1)} collective-permute-done((f32[2,512,25]{1,2,0:T(8,128)S(1)}, f32[2,512,25]{1,2,0:T(8,128)S(1)}, u32[]{:S(2)}, u32[]{:S(2)}) %collective-permute-start.3) | collective-permute-done | bytes 102432 | tf_op jit(solution)/shard_map/ppermute | solution.py:26
  22.5 4.5 %collective-permute-start.5 = (f32[2,25,128]{2,1,0:T(8,128)S(1)}, f32[2,25,128]{2,1,0:T(8,128)S(1)}, u32[]{:S(2)}, u32[]{:S(2)}) collective-permute-start(f32[2,25,128]{2,1,0:T(8,128)S(1)} %get-tuple-element.56), channel_id=1, source_target_pairs={{0,4},{1,5},{2,6},{3,7},{8,12},{9,13},{10,14},{11,15},{16,20},{17,... | collective-permute-start | bytes 76808 | tf_op jit(solution)/shard_map/ppermute | solution.py:24
  28.6 4.2 %collective-permute-done.6 = f32[2,25,128]{2,1,0:T(8,128)S(1)} collective-permute-done((f32[2,25,128]{2,1,0:T(8,128)S(1)}, f32[2,25,128]{2,1,0:T(8,128)S(1)}, u32[]{:S(2)}, u32[]{:S(2)}) %collective-permute-start.6) | collective-permute-done | bytes 25632 | tf_op jit(solution)/shard_map/ppermute | solution.py:26
  33.8 4.0 %collective-permute-start.7 = (f32[2,512,25]{1,2,0:T(8,128)S(1)}, f32[2,512,25]{1,2,0:T(8,128)S(1)}, u32[]{:S(2)}, u32[]{:S(2)}) collective-permute-start(f32[2,512,25]{1,2,0:T(8,128)S(1)} %get-tuple-element.54), channel_id=1, source_target_pairs={{0,1},{1,2},{2,3},{4,5},{5,6},{6,7},{8,9},{9,10},{10,11},{12,13},{... | collective-permute-start | bytes 307208 | tf_op jit(solution)/shard_map/ppermute | solution.py:24
  46.8 4.2 %collective-permute-done.11 = f32[2,25,128]{2,1,0:T(8,128)S(1)} collective-permute-done((f32[2,25,128]{2,1,0:T(8,128)S(1)}, f32[2,25,128]{2,1,0:T(8,128)S(1)}, u32[]{:S(2)}, u32[]{:S(2)}) %collective-permute-start.11) | collective-permute-done | bytes 25632 | tf_op jit(solution)/shard_map/ppermute | solution.py:26
  52.9 3.5 %collective-permute-start.14 = (f32[1,512,128]{2,1,0:T(8,128)S(1)}, f32[1,512,128]{2,1,0:T(8,128)S(1)}, u32[]{:S(2)}, u32[]{:S(2)}) collective-permute-start(f32[1,512,128]{2,1,0:T(8,128)S(1)} %get-tuple-element.46), channel_id=1, source_target_pairs={{0,8},{8,16},{16,24},{1,9},{9,17},{17,25},{2,10},{10,18},{18,26},{... | collective-permute-start | bytes 786440 | tf_op jit(solution)/shard_map/ppermute | solution.py:36
  57.1 4.7 %collective-permute-start.12 = (f32[2,512,25]{1,2,0:T(8,128)}, f32[2,512,25]{1,2,0:T(8,128)}, u32[]{:S(2)}, u32[]{:S(2)}) collective-permute-start(f32[2,512,25]{1,2,0:T(8,128)} %get-tuple-element.50), channel_id=1, source_target_pairs={{0,1},{1,2},{2,3},{4,5},{5,6},{6,7},{8,9},{9,10},{10,11},{12,13},{... | collective-permute-start | bytes 307208 | tf_op jit(solution)/shard_map/ppermute | solution.py:24
  64.3 13.8 %all-reduce.2 = (f32[]{:T(128)}, f32[]{:T(128)}) all-reduce(f32[]{:T(128)S(6)} %add.127, f32[]{:T(128)} %get-tuple-element.26), channel_id=1, replica_groups=mesh['layer'=4,'row'=2,'col'=4] {'row','col'}, use_global_device_ids=true, to_apply=%region_2.3 | all-reduce | flops 2 | bytes 16 | tf_op jit(solution)/shard_map/psum | solution.py:113
  78.1 10.5 %all-reduce.5 = (f32[]{:T(128)}, f32[]{:T(128)}) all-reduce(f32[]{:T(128)} %get-tuple-element.8, f32[]{:T(128)} %get-tuple-element.9), channel_id=1, replica_groups=mesh['layer'=4,'row'=2,'col'=4] {'layer'}, use_global_device_ids=true, to_apply=%region_3.4 | all-reduce | flops 2 | bytes 16 | tf_op jit(solution)/shard_map/psum | solution.py:113
  90.7 3.9 %multiply_reduce_fusion.3 = (f32[]{:T(128)}, f32[2,512,128]{2,1,0:T(8,128)S(1)}, f32[2,512,128]{2,1,0:T(8,128)}) fusion(f32[2,512,128]{2,1,0:T(8,128)} %get-tuple-element.64, f32[2,512,128]{2,1,0:T(8,128)S(1)} %copy-done.1, f32[2,512,128]{2,1,0:T(8,128)S(1)} %get-tuple-element.21, f32[1,512,128]{2,1,0:T(8,128)S(1)} %get-tuple-element.47, ...), kind=kOutput, calls=%fused_computation.139 | convolution fusion | flops 282915840 | bytes 5447688 | tf_op jit(solution)/shard_map/liq,qj->lij/dot_general | solution.py:51
  94.6 4.0 %collective-permute-start.15 = (f32[2,25,128]{2,1,0:T(8,128)S(1)}, f32[2,25,128]{2,1,0:T(8,128)S(1)}, u32[]{:S(2)}, u32[]{:S(2)}) collective-permute-start(f32[2,25,128]{2,1,0:T(8,128)S(1)} %get-tuple-element.44), channel_id=1, source_target_pairs={{0,4},{1,5},{2,6},{3,7},{8,12},{9,13},{10,14},{11,15},{16,20},{17,... | collective-permute-start | bytes 76808 | tf_op jit(solution)/shard_map/ppermute | solution.py:24
  100.2 4.2 %collective-permute-done.16 = f32[2,25,128]{2,1,0:T(8,128)S(1)} collective-permute-done((f32[2,25,128]{2,1,0:T(8,128)S(1)}, f32[2,25,128]{2,1,0:T(8,128)S(1)}, u32[]{:S(2)}, u32[]{:S(2)}) %collective-permute-start.16) | collective-permute-done | bytes 25632 | tf_op jit(solution)/shard_map/ppermute | solution.py:26
  115.0 4.2 %collective-permute-done.21 = f32[2,25,128]{2,1,0:T(8,128)S(1)} collective-permute-done((f32[2,25,128]{2,1,0:T(8,128)S(1)}, f32[2,25,128]{2,1,0:T(8,128)S(1)}, u32[]{:S(2)}, u32[]{:S(2)}) %collective-permute-start.21) | collective-permute-done | bytes 25632 | tf_op jit(solution)/shard_map/ppermute | solution.py:26
  121.1 4.4 %collective-permute-start.24 = (f32[1,512,128]{2,1,0:T(8,128)S(1)}, f32[1,512,128]{2,1,0:T(8,128)S(1)}, u32[]{:S(2)}, u32[]{:S(2)}) collective-permute-start(f32[1,512,128]{2,1,0:T(8,128)S(1)} %get-tuple-element.34), channel_id=1, source_target_pairs={{0,8},{8,16},{16,24},{1,9},{9,17},{17,25},{2,10},{10,18},{18,26},{... | collective-permute-start | bytes 786440 | tf_op jit(solution)/shard_map/ppermute | solution.py:36
  131.0 14.5 %all-reduce.1 = (f32[]{:T(128)}, f32[]{:T(128)}) all-reduce(f32[]{:T(128)S(6)} %add.136, f32[]{:T(128)} %get-tuple-element.24), channel_id=1, replica_groups=mesh['layer'=4,'row'=2,'col'=4] {'row','col'}, use_global_device_ids=true, to_apply=%region_9.10 | all-reduce | flops 2 | bytes 16 | tf_op jit(solution)/shard_map/psum | solution.py:113
  145.5 9.5 %all-reduce.4 = (f32[]{:T(128)}, f32[]{:T(128)}) all-reduce(f32[]{:T(128)} %get-tuple-element.6, f32[]{:T(128)} %get-tuple-element.7), channel_id=1, replica_groups=mesh['layer'=4,'row'=2,'col'=4] {'layer'}, use_global_device_ids=true, to_apply=%region_10.11 | all-reduce | flops 2 | bytes 16 | tf_op jit(solution)/shard_map/psum | solution.py:113
  157.2 3.9 %multiply_reduce_fusion = (f32[]{:T(128)}, f32[2,512,128]{2,1,0:T(8,128)S(1)}, f32[2,512,128]{2,1,0:T(8,128)}) fusion(f32[2,512,128]{2,1,0:T(8,128)} %get-tuple-element.67, f32[2,512,128]{2,1,0:T(8,128)S(1)} %copy-done.1, f32[2,512,128]{2,1,0:T(8,128)S(1)} %get-tuple-element.19, f32[1,512,128]{2,1,0:T(8,128)S(1)} %get-tuple-element.35, ...), kind=kOutput, calls=%fused_computation.134 | convolution fusion | flops 282915840 | bytes 5447688 | tf_op jit(solution)/shard_map/liq,qj->lij/dot_general | solution.py:51
  161.1 4.0 %collective-permute-start.25 = (f32[2,25,128]{2,1,0:T(8,128)S(1)}, f32[2,25,128]{2,1,0:T(8,128)S(1)}, u32[]{:S(2)}, u32[]{:S(2)}) collective-permute-start(f32[2,25,128]{2,1,0:T(8,128)S(1)} %get-tuple-element.32), channel_id=1, source_target_pairs={{0,4},{1,5},{2,6},{3,7},{8,12},{9,13},{10,14},{11,15},{16,20},{17,... | collective-permute-start | bytes 76808 | tf_op jit(solution)/shard_map/ppermute | solution.py:24
  166.7 4.2 %collective-permute-done.26 = f32[2,25,128]{2,1,0:T(8,128)S(1)} collective-permute-done((f32[2,25,128]{2,1,0:T(8,128)S(1)}, f32[2,25,128]{2,1,0:T(8,128)S(1)}, u32[]{:S(2)}, u32[]{:S(2)}) %collective-permute-start.26) | collective-permute-done | bytes 25632 | tf_op jit(solution)/shard_map/ppermute | solution.py:26
  179.0 6.5 %collective-permute-done.29 = f32[1,512,128]{2,1,0:T(8,128)S(1)} collective-permute-done((f32[1,512,128]{2,1,0:T(8,128)S(1)}, f32[1,512,128]{2,1,0:T(8,128)S(1)}, u32[]{:S(2)}, u32[]{:S(2)}) %collective-permute-start.29) | collective-permute-done | bytes 262176 | tf_op jit(solution)/shard_map/ppermute | solution.py:36
  188.3 12.6 %all-reduce = (f32[]{:T(128)}, f32[]{:T(128)}) all-reduce(f32[]{:T(128)S(6)} %add.145, f32[]{:T(128)} %get-tuple-element.22), channel_id=1, replica_groups=mesh['layer'=4,'row'=2,'col'=4] {'row','col'}, use_global_device_ids=true, to_apply=%region_16.17 | all-reduce | flops 2 | bytes 16 | tf_op jit(solution)/shard_map/psum | solution.py:113
  200.9 10.4 %all-reduce.3 = (f32[]{:T(128)}, f32[]{:T(128)}) all-reduce(f32[]{:T(128)} %get-tuple-element.4, f32[]{:T(128)} %get-tuple-element.5), channel_id=1, replica_groups=mesh['layer'=4,'row'=2,'col'=4] {'layer'}, use_global_device_ids=true, to_apply=%region_17.18 | all-reduce | flops 2 | bytes 16 | tf_op jit(solution)/shard_map/psum | solution.py:113
  (111 shorter events, 55.6 us)
Async XLA Ops:
  1.4 11.0 %collective-permute-start = (f32[2,25,128]{2,1,0:T(8,128)S(1)}, f32[2,25,128]{2,1,0:T(8,128)S(1)}, u32[]{:S(2)}, u32[]{:S(2)}) collective-permute-start(f32[2,25,128]{2,1,0:T(8,128)S(1)} %get-tuple-element.62), channel_id=1, source_target_pairs={{0,4},{1,5},{2,6},{3,7},{8,12},{9,13},{10,14},{11,15},{16,20},{17,... | collective-permute-start | bytes 76808 | tf_op jit(solution)/shard_map/ppermute | solution.py:24
  6.3 6.2 %collective-permute-start.1 = (f32[2,25,128]{2,1,0:T(8,128)S(1)}, f32[2,25,128]{2,1,0:T(8,128)S(1)}, u32[]{:S(2)}, u32[]{:S(2)}) collective-permute-start(f32[2,25,128]{2,1,0:T(8,128)S(1)} %get-tuple-element.63), channel_id=1, source_target_pairs={{4,0},{5,1},{6,2},{7,3},{12,8},{13,9},{14,10},{15,11},{20,16},{21,... | collective-permute-start | bytes 76808 | tf_op jit(solution)/shard_map/ppermute | solution.py:26
  8.8 11.1 %collective-permute-start.4 = (f32[1,512,128]{2,1,0:T(8,128)S(1)}, f32[1,512,128]{2,1,0:T(8,128)S(1)}, u32[]{:S(2)}, u32[]{:S(2)}) collective-permute-start(f32[1,512,128]{2,1,0:T(8,128)S(1)} %get-tuple-element.58), channel_id=1, source_target_pairs={{0,8},{8,16},{16,24},{1,9},{9,17},{17,25},{2,10},{10,18},{18,26},{... | collective-permute-start | bytes 786440 | tf_op jit(solution)/shard_map/ppermute | solution.py:36
  14.9 5.0 %collective-permute-start.3 = (f32[2,512,25]{1,2,0:T(8,128)S(1)}, f32[2,512,25]{1,2,0:T(8,128)S(1)}, u32[]{:S(2)}, u32[]{:S(2)}) collective-permute-start(f32[2,512,25]{1,2,0:T(8,128)S(1)} %get-tuple-element.61), channel_id=1, source_target_pairs={{1,0},{2,1},{3,2},{5,4},{6,5},{7,6},{9,8},{10,9},{11,10},{13,12},{... | collective-permute-start | bytes 307208 | tf_op jit(solution)/shard_map/ppermute | solution.py:26
  22.5 6.1 %collective-permute-start.5 = (f32[2,25,128]{2,1,0:T(8,128)S(1)}, f32[2,25,128]{2,1,0:T(8,128)S(1)}, u32[]{:S(2)}, u32[]{:S(2)}) collective-permute-start(f32[2,25,128]{2,1,0:T(8,128)S(1)} %get-tuple-element.56), channel_id=1, source_target_pairs={{0,4},{1,5},{2,6},{3,7},{8,12},{9,13},{10,14},{11,15},{16,20},{17,... | collective-permute-start | bytes 76808 | tf_op jit(solution)/shard_map/ppermute | solution.py:24
  27.0 5.8 %collective-permute-start.6 = (f32[2,25,128]{2,1,0:T(8,128)S(1)}, f32[2,25,128]{2,1,0:T(8,128)S(1)}, u32[]{:S(2)}, u32[]{:S(2)}) collective-permute-start(f32[2,25,128]{2,1,0:T(8,128)S(1)} %get-tuple-element.57), channel_id=1, source_target_pairs={{4,0},{5,1},{6,2},{7,3},{12,8},{13,9},{14,10},{15,11},{20,16},{21,... | collective-permute-start | bytes 76808 | tf_op jit(solution)/shard_map/ppermute | solution.py:26
  33.8 6.7 %collective-permute-start.7 = (f32[2,512,25]{1,2,0:T(8,128)S(1)}, f32[2,512,25]{1,2,0:T(8,128)S(1)}, u32[]{:S(2)}, u32[]{:S(2)}) collective-permute-start(f32[2,512,25]{1,2,0:T(8,128)S(1)} %get-tuple-element.54), channel_id=1, source_target_pairs={{0,1},{1,2},{2,3},{4,5},{5,6},{6,7},{8,9},{9,10},{10,11},{12,13},{... | collective-permute-start | bytes 307208 | tf_op jit(solution)/shard_map/ppermute | solution.py:24
  39.2 12.8 %collective-permute-start.9 = (f32[1,512,128]{2,1,0:T(8,128)S(1)}, f32[1,512,128]{2,1,0:T(8,128)S(1)}, u32[]{:S(2)}, u32[]{:S(2)}) collective-permute-start(f32[1,512,128]{2,1,0:T(8,128)S(1)} %get-tuple-element.49), channel_id=1, source_target_pairs={{8,0},{16,8},{24,16},{9,1},{17,9},{25,17},{10,2},{18,10},{26,18},{... | collective-permute-start | bytes 786440 | tf_op jit(solution)/shard_map/ppermute | solution.py:36
  45.2 5.8 %collective-permute-start.11 = (f32[2,25,128]{2,1,0:T(8,128)S(1)}, f32[2,25,128]{2,1,0:T(8,128)S(1)}, u32[]{:S(2)}, u32[]{:S(2)}) collective-permute-start(f32[2,25,128]{2,1,0:T(8,128)S(1)} %get-tuple-element.53), channel_id=1, source_target_pairs={{4,0},{5,1},{6,2},{7,3},{12,8},{13,9},{14,10},{15,11},{20,16},{21,... | collective-permute-start | bytes 76808 | tf_op jit(solution)/shard_map/ppermute | solution.py:26
  52.9 37.1 %collective-permute-start.14 = (f32[1,512,128]{2,1,0:T(8,128)S(1)}, f32[1,512,128]{2,1,0:T(8,128)S(1)}, u32[]{:S(2)}, u32[]{:S(2)}) collective-permute-start(f32[1,512,128]{2,1,0:T(8,128)S(1)} %get-tuple-element.46), channel_id=1, source_target_pairs={{0,8},{8,16},{16,24},{1,9},{9,17},{17,25},{2,10},{10,18},{18,26},{... | collective-permute-start | bytes 786440 | tf_op jit(solution)/shard_map/ppermute | solution.py:36
  57.1 32.9 %collective-permute-start.12 = (f32[2,512,25]{1,2,0:T(8,128)}, f32[2,512,25]{1,2,0:T(8,128)}, u32[]{:S(2)}, u32[]{:S(2)}) collective-permute-start(f32[2,512,25]{1,2,0:T(8,128)} %get-tuple-element.50), channel_id=1, source_target_pairs={{0,1},{1,2},{2,3},{4,5},{5,6},{6,7},{8,9},{9,10},{10,11},{12,13},{... | collective-permute-start | bytes 307208 | tf_op jit(solution)/shard_map/ppermute | solution.py:24
  61.8 28.2 %collective-permute-start.13 = (f32[2,512,25]{1,2,0:T(8,128)}, f32[2,512,25]{1,2,0:T(8,128)}, u32[]{:S(2)}, u32[]{:S(2)}) collective-permute-start(f32[2,512,25]{1,2,0:T(8,128)} %get-tuple-element.51), channel_id=1, source_target_pairs={{1,0},{2,1},{3,2},{5,4},{6,5},{7,6},{9,8},{10,9},{11,10},{13,12},{... | collective-permute-start | bytes 307208 | tf_op jit(solution)/shard_map/ppermute | solution.py:26
  94.6 5.6 %collective-permute-start.15 = (f32[2,25,128]{2,1,0:T(8,128)S(1)}, f32[2,25,128]{2,1,0:T(8,128)S(1)}, u32[]{:S(2)}, u32[]{:S(2)}) collective-permute-start(f32[2,25,128]{2,1,0:T(8,128)S(1)} %get-tuple-element.44), channel_id=1, source_target_pairs={{0,4},{1,5},{2,6},{3,7},{8,12},{9,13},{10,14},{11,15},{16,20},{17,... | collective-permute-start | bytes 76808 | tf_op jit(solution)/shard_map/ppermute | solution.py:24
  98.6 5.8 %collective-permute-start.16 = (f32[2,25,128]{2,1,0:T(8,128)S(1)}, f32[2,25,128]{2,1,0:T(8,128)S(1)}, u32[]{:S(2)}, u32[]{:S(2)}) collective-permute-start(f32[2,25,128]{2,1,0:T(8,128)S(1)} %get-tuple-element.45), channel_id=1, source_target_pairs={{4,0},{5,1},{6,2},{7,3},{12,8},{13,9},{14,10},{15,11},{20,16},{21,... | collective-permute-start | bytes 76808 | tf_op jit(solution)/shard_map/ppermute | solution.py:26
  105.4 4.1 %collective-permute-start.17 = (f32[2,512,25]{1,2,0:T(8,128)S(1)}, f32[2,512,25]{1,2,0:T(8,128)S(1)}, u32[]{:S(2)}, u32[]{:S(2)}) collective-permute-start(f32[2,512,25]{1,2,0:T(8,128)S(1)} %get-tuple-element.42), channel_id=1, source_target_pairs={{0,1},{1,2},{2,3},{4,5},{5,6},{6,7},{8,9},{9,10},{10,11},{12,13},{... | collective-permute-start | bytes 307208 | tf_op jit(solution)/shard_map/ppermute | solution.py:24
  108.2 12.0 %collective-permute-start.19 = (f32[1,512,128]{2,1,0:T(8,128)S(1)}, f32[1,512,128]{2,1,0:T(8,128)S(1)}, u32[]{:S(2)}, u32[]{:S(2)}) collective-permute-start(f32[1,512,128]{2,1,0:T(8,128)S(1)} %get-tuple-element.37), channel_id=1, source_target_pairs={{8,0},{16,8},{24,16},{9,1},{17,9},{25,17},{10,2},{18,10},{26,18},{... | collective-permute-start | bytes 786440 | tf_op jit(solution)/shard_map/ppermute | solution.py:36
  113.4 5.8 %collective-permute-start.21 = (f32[2,25,128]{2,1,0:T(8,128)S(1)}, f32[2,25,128]{2,1,0:T(8,128)S(1)}, u32[]{:S(2)}, u32[]{:S(2)}) collective-permute-start(f32[2,25,128]{2,1,0:T(8,128)S(1)} %get-tuple-element.41), channel_id=1, source_target_pairs={{4,0},{5,1},{6,2},{7,3},{12,8},{13,9},{14,10},{15,11},{20,16},{21,... | collective-permute-start | bytes 76808 | tf_op jit(solution)/shard_map/ppermute | solution.py:26
  121.1 35.3 %collective-permute-start.24 = (f32[1,512,128]{2,1,0:T(8,128)S(1)}, f32[1,512,128]{2,1,0:T(8,128)S(1)}, u32[]{:S(2)}, u32[]{:S(2)}) collective-permute-start(f32[1,512,128]{2,1,0:T(8,128)S(1)} %get-tuple-element.34), channel_id=1, source_target_pairs={{0,8},{8,16},{16,24},{1,9},{9,17},{17,25},{2,10},{10,18},{18,26},{... | collective-permute-start | bytes 786440 | tf_op jit(solution)/shard_map/ppermute | solution.py:36
  126.2 30.2 %collective-permute-start.22 = (f32[2,512,25]{1,2,0:T(8,128)}, f32[2,512,25]{1,2,0:T(8,128)}, u32[]{:S(2)}, u32[]{:S(2)}) collective-permute-start(f32[2,512,25]{1,2,0:T(8,128)} %get-tuple-element.38), channel_id=1, source_target_pairs={{0,1},{1,2},{2,3},{4,5},{5,6},{6,7},{8,9},{9,10},{10,11},{12,13},{... | collective-permute-start | bytes 307208 | tf_op jit(solution)/shard_map/ppermute | solution.py:24
  128.5 27.9 %collective-permute-start.23 = (f32[2,512,25]{1,2,0:T(8,128)}, f32[2,512,25]{1,2,0:T(8,128)}, u32[]{:S(2)}, u32[]{:S(2)}) collective-permute-start(f32[2,512,25]{1,2,0:T(8,128)} %get-tuple-element.39), channel_id=1, source_target_pairs={{1,0},{2,1},{3,2},{5,4},{6,5},{7,6},{9,8},{10,9},{11,10},{13,12},{... | collective-permute-start | bytes 307208 | tf_op jit(solution)/shard_map/ppermute | solution.py:26
  161.1 5.6 %collective-permute-start.25 = (f32[2,25,128]{2,1,0:T(8,128)S(1)}, f32[2,25,128]{2,1,0:T(8,128)S(1)}, u32[]{:S(2)}, u32[]{:S(2)}) collective-permute-start(f32[2,25,128]{2,1,0:T(8,128)S(1)} %get-tuple-element.32), channel_id=1, source_target_pairs={{0,4},{1,5},{2,6},{3,7},{8,12},{9,13},{10,14},{11,15},{16,20},{17,... | collective-permute-start | bytes 76808 | tf_op jit(solution)/shard_map/ppermute | solution.py:24
  165.1 5.8 %collective-permute-start.26 = (f32[2,25,128]{2,1,0:T(8,128)S(1)}, f32[2,25,128]{2,1,0:T(8,128)S(1)}, u32[]{:S(2)}, u32[]{:S(2)}) collective-permute-start(f32[2,25,128]{2,1,0:T(8,128)S(1)} %get-tuple-element.33), channel_id=1, source_target_pairs={{4,0},{5,1},{6,2},{7,3},{12,8},{13,9},{14,10},{15,11},{20,16},{21,... | collective-permute-start | bytes 76808 | tf_op jit(solution)/shard_map/ppermute | solution.py:26
  171.8 4.1 %collective-permute-start.27 = (f32[2,512,25]{1,2,0:T(8,128)S(1)}, f32[2,512,25]{1,2,0:T(8,128)S(1)}, u32[]{:S(2)}, u32[]{:S(2)}) collective-permute-start(f32[2,512,25]{1,2,0:T(8,128)S(1)} %get-tuple-element.30), channel_id=1, source_target_pairs={{0,1},{1,2},{2,3},{4,5},{5,6},{6,7},{8,9},{9,10},{10,11},{12,13},{... | collective-permute-start | bytes 307208 | tf_op jit(solution)/shard_map/ppermute | solution.py:24
  174.6 10.9 %collective-permute-start.29 = (f32[1,512,128]{2,1,0:T(8,128)S(1)}, f32[1,512,128]{2,1,0:T(8,128)S(1)}, u32[]{:S(2)}, u32[]{:S(2)}) collective-permute-start(f32[1,512,128]{2,1,0:T(8,128)S(1)} %get-tuple-element.29), channel_id=1, source_target_pairs={{8,0},{16,8},{24,16},{9,1},{17,9},{25,17},{10,2},{18,10},{26,18},{... | collective-permute-start | bytes 786440 | tf_op jit(solution)/shard_map/ppermute | solution.py:36
  (22 other events, 136.0 us)
